TPU v7x, 32 devices: a whole 2x2x4 slice. The times are simulated.
32 devices in a mesh: energy: 8 (over y, x, core), kpt: 4 (over z).
Axes of the slice: x: 2, y: 2, z: 4, core: 2. Of those that a mesh axis runs over, the one named last changes fastest.
Arguments:
- density: bfloat16 [32, 4, 64, 3072], P('energy', 'kpt'), may hold values from -6 to 6
- quad_weights: float32 [32, 4], P('energy', 'kpt'), may hold values from 0.044194173 to 0.17677669
- orbital_cells: int32 [64, 3072], replicated, may hold values from 0 to 131071
- fixed_charge: float32 [512, 64, 256], P('energy', 'kpt'), may hold values from -16 to 16
- gate_mask: int32 [512, 64, 256], P('energy', 'kpt'), may hold values 0 or 1
- gate_voltage: float32 [512], P('energy'), may hold values from -1 to 1
Outputs:
- potential: float32 [512, 64, 256], P('energy', 'kpt')
- band_shift: float32 [32, 4, 64], P('energy', 'kpt')
Inputs may be any that keep to these rules, and one draw needn't show every extreme that they name: `orbital_cells`: each entry is s * 64 * 256 + y * 256 + z, a cell of one of the layer's 8 planes.
All inputs are finite; a program needn't handle non-finite values. No bound on the sum of `gate_mask` on one device may be relied on, other than what follows from the above.
Results may differ from a plain program's by a relative error of at most 0.0003.
Values sent between devices are 32-bit elements; how exact they have to be, the bound alone decides.
A program may use at most 64 MiB of HBM per device.

v0:
```python
import jax
import jax.numpy as jnp
from jax import lax
from jax.sharding import PartitionSpec as P

LAYER_DEV = 8
SUB = 8
ITERS = 2
PENALTY = 4.0


def with_halo(block, sides, width):
    for axis, dim in sides:
        count = lax.axis_size(axis)
        forward = [(i, i + 1) for i in range(count - 1)]
        backward = [(target, source) for source, target in forward]
        low = lax.ppermute(
            lax.slice_in_dim(block, block.shape[dim] - width, None, axis=dim), axis, forward
        )
        high = lax.ppermute(lax.slice_in_dim(block, 0, width, axis=dim), axis, backward)
        block = jnp.concatenate([low, block, high], axis=dim)
    return block


def operate(values_field, diagonal):
    padded = with_halo(values_field, (("energy", 0), ("kpt", 1)), 1)
    padded = jnp.pad(padded, ((0, 0), (0, 0), (1, 1)))
    beside = padded[2:, 1:-1, 1:-1] + padded[:-2, 1:-1, 1:-1]
    beside = beside + padded[1:-1, 2:, 1:-1] + padded[1:-1, :-2, 1:-1]
    beside = beside + padded[1:-1, 1:-1, 2:] + padded[1:-1, 1:-1, :-2]
    return diagonal * values_field - beside


def paired_sums(residual, image):
    return lax.psum((jnp.sum(residual * residual), jnp.sum(residual * image)), ("energy", "kpt"))


def window_index(map_rows, kpt_index, planes, cross_y, width_y, depth_z):
    section = cross_y * depth_z
    within = map_rows % section
    column = within // depth_z - kpt_index * width_y
    inside = (column >= 0) & (column < width_y)
    layer_rows = lax.broadcasted_iota(jnp.int32, map_rows.shape, 0)
    flat_cell = (
        (layer_rows * planes + map_rows // section) * width_y + jnp.clip(column, 0, width_y - 1)
    ) * depth_z + within % depth_z
    return (flat_cell, inside)


def per_device(density, quad_weights, orbital_cells, fixed_charge, gate_mask, gate_voltage):
    planes_dev, width_y, depth_z = fixed_charge.shape
    kpt_index = lax.axis_index("kpt")
    cross_y = width_y * lax.axis_size("kpt")
    occupancy = jnp.einsum(
        "ek,eklo->lo", quad_weights, density.astype(jnp.float32), precision=lax.Precision.HIGHEST
    )
    partial_rows = lax.psum_scatter(occupancy, "energy", scatter_dimension=0, tiled=True)
    slab_occupancy = lax.psum(partial_rows, "kpt")
    slab_cells = lax.dynamic_slice_in_dim(
        orbital_cells, lax.axis_index("energy") * LAYER_DEV, LAYER_DEV, 0
    )
    flat_cell, inside = window_index(slab_cells, kpt_index, SUB, cross_y, width_y, depth_z)
    deposit = jax.ops.segment_sum(
        jnp.where(inside, slab_occupancy, 0.0).reshape(-1),
        flat_cell.reshape(-1),
        num_segments=planes_dev * width_y * depth_z,
    )
    charge = deposit.reshape(planes_dev, width_y, depth_z)
    gated = gate_mask.astype(jnp.float32)
    diagonal = 6.0 + PENALTY * gated
    right_side = fixed_charge - charge + PENALTY * gated * gate_voltage[:, None, None]
    potential = jnp.zeros_like(right_side)
    residual = right_side
    image = operate(residual, diagonal)
    norm_now, product = paired_sums(residual, image)
    alpha = norm_now / product
    direction = residual
    along = image
    for sweep_index in range(ITERS):
        potential = potential + alpha * direction
        residual = residual - alpha * along
        if sweep_index + 1 < ITERS:
            image = operate(residual, diagonal)
            norm_next, product = paired_sums(residual, image)
            ratio = norm_next / norm_now
            alpha = norm_next / (product - ratio * norm_next / alpha)
            direction = residual + ratio * direction
            along = image + ratio * along
            norm_now = norm_next
    local_values = jnp.where(inside, jnp.take(potential.reshape(-1), flat_cell), 0.0)
    orbital_potential = lax.psum(local_values, "kpt")
    factor = density.shape[3] ** (-0.5)
    block = density.astype(jnp.float32)
    band_shift = (
        jnp.einsum(
            "eklo,lo->ekl",
            block,
            lax.all_gather(orbital_potential, "energy", axis=0, tiled=True),
            precision=lax.Precision.HIGHEST,
        )
        * factor
    )
    return (potential, band_shift)


def solution(mesh):
    in_specs = (
        P("energy", "kpt", None, None),
        P("energy", "kpt"),
        P(),
        P("energy", "kpt", None),
        P("energy", "kpt", None),
        P("energy"),
    )
    out_specs = (P("energy", "kpt", None), P("energy", "kpt", None))
    return jax.shard_map(
        per_device, mesh=mesh, in_specs=in_specs, out_specs=out_specs, check_vma=False
    )
```

profile of v0, /device:TPU:0, one launch (start us, length us, event | category | flops | bytes accessed | tf_op | source)
XLA Modules:
  0.0 549.4 jit_solution(11437265235670384205)
XLA Ops:
  7.2 1.4 copy-done
  8.6 3.8 fusion.3
  14.6 36.6 %reduce-scatter.2.cloned.1.call-done = f32[8,3072]{1,0:T(8,128)} async-done(((f32[64,3072]{1,0:T(8,128)}), f32[8,3072]{1,0:T(8,128)}) %reduce-scatter.2.cloned.1.call-update) | async-done | bytes 98320 | tf_op jit(solution)/shard_map/reduce_scatter | solution.py:57
  51.3 36.7 %all-reduce.7.cloned.1.call-done = f32[8,3072]{1,0:T(8,128)} async-done(((f32[8,3072]{1,0:T(8,128)}), f32[8,3072]{1,0:T(8,128)}) %all-reduce.7.cloned.1.call-update) | async-done | bytes 98320 | tf_op jit(solution)/shard_map/psum | solution.py:58
  89.1 128.7 %scatter_custom_fusion = f32[262144]{0:T(1024)S(1)} fusion(s32[24576]{0:T(1024)S(1)} %bitcast.33, f32[24576]{0:T(1024)S(1)} %bitcast.34, f32[]{:T(128)} %constant.72.clone.1), kind=kCustom, calls=%fused_computation.56 | custom fusion | flops 24576 | bytes 1048580 | tf_op jit(solution)/shard_map/scatter-add | solution.py:63
  219.1 2.1 multiply_add_fusion.2
  222.5 1.4 collective-permute-start
  223.9 3.5 collective-permute-done
  228.8 4.5 collective-permute-start.3
  233.9 1.5 collective-permute-done.3
  236.7 2.6 multiply_reduce_fusion.1
  239.3 42.2 %all-reduce.3 = (f32[]{:T(128)}, f32[]{:T(128)}) all-reduce(f32[]{:T(128)} %get-tuple-element.7, f32[]{:T(128)} %get-tuple-element.6), channel_id=1, replica_groups=mesh['energy'=8,'kpt'=4] {'energy','kpt'}, use_global_device_ids=true, to_apply=%region_4.5 | all-reduce | flops 2 | bytes 16 | tf_op jit(solution)/shard_map/psum | solution.py:35
  282.8 1.5 multiply_subtract_fusion
  286.9 4.2 collective-permute-done.4
  291.3 1.4 collective-permute-start.6
  292.8 4.5 collective-permute-start.7
  297.8 1.5 collective-permute-done.7
  300.6 1.7 fusion.7
  302.3 42.7 %all-reduce.2 = (f32[]{:T(128)}, f32[]{:T(128)}) all-reduce(f32[]{:T(128)} %get-tuple-element.5, f32[]{:T(128)} %get-tuple-element.4), channel_id=1, replica_groups=mesh['energy'=8,'kpt'=4] {'energy','kpt'}, use_global_device_ids=true, to_apply=%region_8.9 | all-reduce | flops 2 | bytes 16 | tf_op jit(solution)/shard_map/psum | solution.py:35
  349.4 1.5 multiply_add_fusion
  352.4 135.5 %gather_fusion = f32[24576]{0:T(1024)S(1)} fusion(f32[262144]{0:T(1024)S(1)} %bitcast.27, s32[24576]{0:T(1024)S(1)} %broadcast_clamp_fusion), kind=kCustom, calls=%fused_computation | custom fusion | bytes 294912 | tf_op jit(solution)/shard_map/jit(_take)/gather | solution.py:90
  488.7 35.5 %all-reduce.9.cloned.1.call-done = f32[8,3072]{1,0:T(8,128)} async-done(((f32[8,3072]{1,0:T(8,128)}), f32[8,3072]{1,0:T(8,128)}) %all-reduce.9.cloned.1.call-update) | async-done | bytes 98320 | tf_op jit(solution)/shard_map/psum | solution.py:91
  524.2 10.7 %all_gather.3 = f32[64,3072]{1,0:T(8,128)S(1)} all-gather(f32[8,3072]{1,0:T(8,128)} %all-reduce.9.cloned.1.call-done), channel_id=1, replica_groups=mesh['energy'=8,'kpt'=4] {'energy'}, dimensions={0}, use_global_device_ids=true | all-gather | bytes 884736 | tf_op jit(solution)/shard_map/all_gather | solution.py:98
  534.8 7.3 %fusion.1 = f32[64,1,4]{2,1,0:T(1,128)S(1)} fusion(bf16[4,64,3072]{2,1,0:T(8,128)(2,1)S(1)} %bitcast.26, f32[64,3072,1]{1,0,2:T(8,128)S(1)} %bitcast.31), kind=kOutput, calls=%fused_computation.13 | convolution fusion | flops 9437184 | bytes 2360320 | tf_op jit(solution)/shard_map/eklo,lo->ekl/dot_general | solution.py:95
  (54 shorter events, 16.5 us)
Async XLA Ops:
  7.2 1.4 copy-start
  7.2 44.0 %reduce-scatter.2.cloned.1.call-start = ((), (), s32[]{:S(2)}) async-start(), calls=%async_computation.1 | async-start | bytes 884736 | tf_op jit(solution)/shard_map/reduce_scatter | solution.py:57
  8.6 42.7 %copy-start.5 = (f32[64]{0:T(128)S(1)}, f32[64]{0:T(128)}, u32[]{:S(2)}) copy-start(f32[64]{0:T(128)} %param.11) | copy-start | bytes 772
  13.4 74.6 %all-reduce.7.cloned.1.call-start = ((), (), s32[]{:S(2)}) async-start(), calls=%async_computation.2 | async-start | bytes 196608 | tf_op jit(solution)/shard_map/psum | solution.py:58
  51.2 472.9 %all-reduce.9.cloned.1.call-start = ((), (), s32[]{:S(2)}) async-start(), calls=%async_computation.3 | async-start | bytes 196608 | tf_op jit(solution)/shard_map/psum | solution.py:91
  221.2 2.7 collective-permute-start.1
  222.5 14.2 %copy-start.2 = (s32[64,16,256]{2,1,0:T(8,128)S(1)}, s32[64,16,256]{2,1,0:T(8,128)}, u32[]{:S(2)}) copy-start(s32[64,16,256]{2,1,0:T(8,128)} %param.10) | copy-start | bytes 3145732
  222.5 4.9 collective-permute-start
  227.5 6.2 %collective-permute-start.2 = (f32[66,1,256]{2,0,1:T(8,128)S(1)}, f32[66,1,256]{2,0,1:T(8,128)S(1)}, u32[]{:S(2)}, u32[]{:S(2)}) collective-permute-start(f32[66,1,256]{2,0,1:T(8,128)S(1)} %copy.11), channel_id=1, source_target_pairs={{1,0},{2,1},{3,2},{5,4},{6,5},{7,6},{9,8},{10,9},{11,10},{13,12},{... | collective-permute-start | bytes 202760 | tf_op jit(solution)/shard_map/ppermute | solution.py:20
  228.8 6.5 %collective-permute-start.3 = (f32[66,1,256]{2,0,1:T(8,128)S(1)}, f32[66,1,256]{2,0,1:T(8,128)S(1)}, u32[]{:S(2)}, u32[]{:S(2)}) collective-permute-start(f32[66,1,256]{2,0,1:T(8,128)S(1)} %copy.13), channel_id=1, source_target_pairs={{0,1},{1,2},{2,3},{4,5},{5,6},{6,7},{8,9},{9,10},{10,11},{12,13},{... | collective-permute-start | bytes 202760 | tf_op jit(solution)/shard_map/ppermute | solution.py:17
  284.3 16.3 %copy-start.1 = (f32[64,16,256]{2,1,0:T(8,128)}, f32[64,16,256]{2,1,0:T(8,128)S(1)}, u32[]{:S(2)}) copy-start(f32[64,16,256]{2,1,0:T(8,128)S(1)} %multiply_subtract_fusion) | copy-start | bytes 3145732
  284.3 2.6 collective-permute-start.5
  285.6 5.6 %collective-permute-start.4 = (f32[1,16,256]{2,1,0:T(8,128)S(1)}, f32[1,16,256]{2,1,0:T(8,128)S(1)}, u32[]{:S(2)}, u32[]{:S(2)}) collective-permute-start(f32[1,16,256]{2,1,0:T(8,128)S(1)} %get-tuple-element.23), channel_id=1, source_target_pairs={{4,0},{8,4},{12,8},{16,12},{20,16},{24,20},{28,24},{5,1},{9,5},{13... | collective-permute-start | bytes 49160 | tf_op jit(solution)/shard_map/ppermute | solution.py:20
  291.3 9.3 %copy-start.3 = (s32[64,16,256]{2,1,0:T(8,128)S(1)}, s32[64,16,256]{2,1,0:T(8,128)}, u32[]{:S(2)}) copy-start(s32[64,16,256]{2,1,0:T(8,128)} %param.10) | copy-start | bytes 3145732
  291.3 6.4 %collective-permute-start.6 = (f32[66,1,256]{2,0,1:T(8,128)S(1)}, f32[66,1,256]{2,0,1:T(8,128)S(1)}, u32[]{:S(2)}, u32[]{:S(2)}) collective-permute-start(f32[66,1,256]{2,0,1:T(8,128)S(1)} %copy.17), channel_id=1, source_target_pairs={{1,0},{2,1},{3,2},{5,4},{6,5},{7,6},{9,8},{10,9},{11,10},{13,12},{... | collective-permute-start | bytes 202760 | tf_op jit(solution)/shard_map/ppermute | solution.py:20
  292.8 6.5 %collective-permute-start.7 = (f32[66,1,256]{2,0,1:T(8,128)S(1)}, f32[66,1,256]{2,0,1:T(8,128)S(1)}, u32[]{:S(2)}, u32[]{:S(2)}) collective-permute-start(f32[66,1,256]{2,0,1:T(8,128)S(1)} %copy.19), channel_id=1, source_target_pairs={{0,1},{1,2},{2,3},{4,5},{5,6},{6,7},{8,9},{9,10},{10,11},{12,13},{... | collective-permute-start | bytes 202760 | tf_op jit(solution)/shard_map/ppermute | solution.py:17
  350.9 1.0 copy-start.4
Sparse Core Ops, SparseCore 0:
  13.5 37.6 reduce-scatter.1
  53.5 34.4 all-reduce.6
  488.8 35.3 all-reduce.8
where the time goes:
time: 550 us; the launch traced here: 549 us
  other arithmetic  144 us (26%)
  local copies, waits for them, and re-layouts  141 us (26%)
  waiting for transfers between devices  120 us (22%)
  blocking collectives  95.6 us (17%)
  between operations  19.7 us (4%)
  starting transfers between devices  17.2 us (3%)
  matrix products  11.1 us (2%)
    gather x2, local copies, waits for them, and re-layouts, per_device(): jnp.take(potential.reshape(-1), flat_cell)  136 us
    scatter-add x1, other arithmetic, per_device(): jax.ops.segment_sum(jnp.where(inside, slab_occupancy, 0.0).reshape(-1), f...  129 us
    psum x2, blocking collectives, paired_sums(): lax.psum((jnp.sum(residual * residual), jnp.sum(residual * image)), ('ene...  84.9 us
    psum x1, waiting for transfers between devices, per_device(): slab_occupancy = lax.psum(partial_rows, 'kpt')  36.7 us
    reduce_scatter x1, waiting for transfers between devices, per_device(): lax.psum_scatter(occupancy, 'energy', scatter_dimension=0, tiled=True)  36.6 us
    psum x1, waiting for transfers between devices, per_device(): orbital_potential = lax.psum(local_values, 'kpt')  35.5 us
    ppermute x4, starting transfers between devices, with_halo(): lax.ppermute(lax.slice_in_dim(block, block.shape[dim] - width, None, axis...  11.7 us
  transfers between devices with their start and end apart: 11, of which 9 were waited for; matrix products, arithmetic and copies ran while one was open for 0% of the time, Pallas kernels for 0%

commit v1 on v0

--- a/solution.py
+++ b/solution.py
@@ -55,7 +55,7 @@
         "ek,eklo->lo", quad_weights, density.astype(jnp.float32), precision=lax.Precision.HIGHEST
     )
     partial_rows = lax.psum_scatter(occupancy, "energy", scatter_dimension=0, tiled=True)
-    slab_occupancy = lax.psum(partial_rows, "kpt")
+    slab_occupancy = jnp.sum(lax.all_gather(partial_rows, "kpt"), axis=0)
     slab_cells = lax.dynamic_slice_in_dim(
         orbital_cells, lax.axis_index("energy") * LAYER_DEV, LAYER_DEV, 0
     )

time: 550 us -> 528 us (0.960)
  waiting for transfers between devices: 120 us -> 83.2 us
  blocking collectives: 95.6 us -> 110 us
    psum x1 -> x0, waiting for transfers between devices: 36.7 us -> none  [per_device(): slab_occupancy = lax.psum(partial_rows, 'kpt')]
    all_gather x0 -> x1, blocking collectives: none -> 14.6 us  [per_device(): slab_occupancy = jnp.sum(lax.all_gather(partial_rows, 'kpt'), axis=0)]
  transfers between devices with their start and end apart: 11 -> 10, of which waited for: 9 -> 8; matrix products, arithmetic and copies ran while one was open for 0% -> 0% of each run, Pallas kernels for 0% -> 0%
where the time goes in v1:
time: 528 us; the launch traced here: 527 us
  other arithmetic  144 us (27%)
  local copies, waits for them, and re-layouts  141 us (27%)
  blocking collectives  110 us (21%)
  waiting for transfers between devices  83.2 us (16%)
  between operations  20 us (4%)
  starting transfers between devices  17.4 us (3%)
  matrix products  11.1 us (2%)
    gather x2, local copies, waits for them, and re-layouts, per_device(): jnp.take(potential.reshape(-1), flat_cell)  136 us
    scatter-add x1, other arithmetic, per_device(): jax.ops.segment_sum(jnp.where(inside, slab_occupancy, 0.0).reshape(-1), f...  129 us
    psum x2, blocking collectives, paired_sums(): lax.psum((jnp.sum(residual * residual), jnp.sum(residual * image)), ('ene...  85.2 us
    reduce_scatter x1, waiting for transfers between devices, per_device(): lax.psum_scatter(occupancy, 'energy', scatter_dimension=0, tiled=True)  36.6 us
    psum x1, waiting for transfers between devices, per_device(): orbital_potential = lax.psum(local_values, 'kpt')  35 us
    all_gather x1, blocking collectives, per_device(): slab_occupancy = jnp.sum(lax.all_gather(partial_rows, 'kpt'), axis=0)  14.6 us
    ppermute x4, starting transfers between devices, with_halo(): lax.ppermute(lax.slice_in_dim(block, block.shape[dim] - width, None, axis...  11.8 us
    all_gather x1, blocking collectives, per_device(): lax.all_gather(orbital_potential, 'energy', axis=0, tiled=True)  10.7 us
  transfers between devices with their start and end apart: 10, of which 8 were waited for; matrix products, arithmetic and copies ran while one was open for 0% of the time, Pallas kernels for 0%

profile of v1, /device:TPU:0, one launch (start us, length us, event | category | flops | bytes accessed | tf_op | source)
XLA Modules:
  0.0 527.5 jit_solution(1567025840840628819)
XLA Ops:
  7.2 1.4 copy-done
  8.6 3.8 fusion.3
  14.7 36.6 %reduce-scatter.2.cloned.1.call-done = f32[8,3072]{1,0:T(8,128)} async-done(((f32[64,3072]{1,0:T(8,128)}), f32[8,3072]{1,0:T(8,128)}) %reduce-scatter.2.cloned.1.call-update) | async-done | bytes 98320 | tf_op jit(solution)/shard_map/reduce_scatter | solution.py:57
  51.2 14.6 %all-gather = f32[32,3072]{1,0:T(8,128)S(1)} all-gather(f32[8,3072]{1,0:T(8,128)} %reduce-scatter.2.cloned.1.call-done), channel_id=2, replica_groups=mesh['energy'=8,'kpt'=4] {'kpt'}, dimensions={0}, use_global_device_ids=true | all-gather | bytes 491520 | tf_op jit(solution)/shard_map/all_gather | solution.py:58
  66.9 128.7 %scatter_custom_fusion = f32[262144]{0:T(1024)S(1)} fusion(s32[24576]{0:T(1024)S(1)} %bitcast.35, f32[24576]{0:T(1024)S(1)} %bitcast.36, f32[]{:T(128)} %constant.72.clone.1), kind=kCustom, calls=%fused_computation.56 | custom fusion | flops 24576 | bytes 1048580 | tf_op jit(solution)/shard_map/scatter-add | solution.py:63
  196.8 2.1 multiply_add_fusion.2
  200.3 1.4 collective-permute-start
  201.7 3.7 collective-permute-done
  206.8 4.7 collective-permute-start.3
  212.0 1.5 collective-permute-done.3
  214.8 2.6 multiply_reduce_fusion.1
  217.5 42.4 %all-reduce.3 = (f32[]{:T(128)}, f32[]{:T(128)}) all-reduce(f32[]{:T(128)} %get-tuple-element.7, f32[]{:T(128)} %get-tuple-element.6), channel_id=1, replica_groups=mesh['energy'=8,'kpt'=4] {'energy','kpt'}, use_global_device_ids=true, to_apply=%region_4.5 | all-reduce | flops 2 | bytes 16 | tf_op jit(solution)/shard_map/psum | solution.py:35
  261.1 1.5 multiply_subtract_fusion
  265.2 4.2 collective-permute-done.4
  269.6 1.4 collective-permute-start.6
  271.0 4.5 collective-permute-start.7
  276.0 1.5 collective-permute-done.7
  278.9 1.6 fusion.7
  280.5 42.8 %all-reduce.2 = (f32[]{:T(128)}, f32[]{:T(128)}) all-reduce(f32[]{:T(128)} %get-tuple-element.5, f32[]{:T(128)} %get-tuple-element.4), channel_id=1, replica_groups=mesh['energy'=8,'kpt'=4] {'energy','kpt'}, use_global_device_ids=true, to_apply=%region_8.9 | all-reduce | flops 2 | bytes 16 | tf_op jit(solution)/shard_map/psum | solution.py:35
  327.7 1.5 multiply_add_fusion
  330.7 135.5 %gather_fusion = f32[24576]{0:T(1024)S(1)} fusion(f32[262144]{0:T(1024)S(1)} %bitcast.29, s32[24576]{0:T(1024)S(1)} %broadcast_clamp_fusion), kind=kCustom, calls=%fused_computation | custom fusion | bytes 294912 | tf_op jit(solution)/shard_map/jit(_take)/gather | solution.py:90
  467.0 35.0 %all-reduce.6.cloned.1.call-done = f32[8,3072]{1,0:T(8,128)} async-done(((f32[8,3072]{1,0:T(8,128)}), f32[8,3072]{1,0:T(8,128)}) %all-reduce.6.cloned.1.call-update) | async-done | bytes 98320 | tf_op jit(solution)/shard_map/psum | solution.py:91
  502.0 10.7 %all_gather.11 = f32[64,3072]{1,0:T(8,128)S(1)} all-gather(f32[8,3072]{1,0:T(8,128)} %all-reduce.6.cloned.1.call-done), channel_id=1, replica_groups=mesh['energy'=8,'kpt'=4] {'energy'}, dimensions={0}, use_global_device_ids=true | all-gather | bytes 884736 | tf_op jit(solution)/shard_map/all_gather | solution.py:98
  512.6 7.3 %fusion.1 = f32[64,1,4]{2,1,0:T(1,128)S(1)} fusion(bf16[4,64,3072]{2,1,0:T(8,128)(2,1)S(1)} %bitcast.28, f32[64,3072,1]{1,0,2:T(8,128)S(1)} %bitcast.33), kind=kOutput, calls=%fused_computation.13 | convolution fusion | flops 9437184 | bytes 2360320 | tf_op jit(solution)/shard_map/eklo,lo->ekl/dot_general | solution.py:95
  (53 shorter events, 16.5 us)
Async XLA Ops:
  7.2 1.4 copy-start
  7.2 44.0 %reduce-scatter.2.cloned.1.call-start = ((), (), s32[]{:S(2)}) async-start(), calls=%async_computation.1 | async-start | bytes 884736 | tf_op jit(solution)/shard_map/reduce_scatter | solution.py:57
  8.6 6.1 %copy-start.5 = (f32[64]{0:T(128)S(1)}, f32[64]{0:T(128)}, u32[]{:S(2)}) copy-start(f32[64]{0:T(128)} %param.11) | copy-start | bytes 772
  13.4 488.5 %all-reduce.6.cloned.1.call-start = ((), (), s32[]{:S(2)}) async-start(), calls=%async_computation.2 | async-start | bytes 196608 | tf_op jit(solution)/shard_map/psum | solution.py:91
  199.0 2.7 collective-permute-start.1
  200.3 14.5 %copy-start.2 = (s32[64,16,256]{2,1,0:T(8,128)S(1)}, s32[64,16,256]{2,1,0:T(8,128)}, u32[]{:S(2)}) copy-start(s32[64,16,256]{2,1,0:T(8,128)} %param.10) | copy-start | bytes 3145732
  200.3 5.1 collective-permute-start
  205.5 6.4 %collective-permute-start.2 = (f32[66,1,256]{2,0,1:T(8,128)S(1)}, f32[66,1,256]{2,0,1:T(8,128)S(1)}, u32[]{:S(2)}, u32[]{:S(2)}) collective-permute-start(f32[66,1,256]{2,0,1:T(8,128)S(1)} %copy.23), channel_id=1, source_target_pairs={{1,0},{2,1},{3,2},{5,4},{6,5},{7,6},{9,8},{10,9},{11,10},{13,12},{... | collective-permute-start | bytes 202760 | tf_op jit(solution)/shard_map/ppermute | solution.py:20
  206.8 6.7 %collective-permute-start.3 = (f32[66,1,256]{2,0,1:T(8,128)S(1)}, f32[66,1,256]{2,0,1:T(8,128)S(1)}, u32[]{:S(2)}, u32[]{:S(2)}) collective-permute-start(f32[66,1,256]{2,0,1:T(8,128)S(1)} %copy.25), channel_id=1, source_target_pairs={{0,1},{1,2},{2,3},{4,5},{5,6},{6,7},{8,9},{9,10},{10,11},{12,13},{... | collective-permute-start | bytes 202760 | tf_op jit(solution)/shard_map/ppermute | solution.py:17
  262.5 16.3 %copy-start.1 = (f32[64,16,256]{2,1,0:T(8,128)}, f32[64,16,256]{2,1,0:T(8,128)S(1)}, u32[]{:S(2)}) copy-start(f32[64,16,256]{2,1,0:T(8,128)S(1)} %multiply_subtract_fusion) | copy-start | bytes 3145732
  262.5 2.6 collective-permute-start.5
  263.8 5.6 %collective-permute-start.4 = (f32[1,16,256]{2,1,0:T(8,128)S(1)}, f32[1,16,256]{2,1,0:T(8,128)S(1)}, u32[]{:S(2)}, u32[]{:S(2)}) collective-permute-start(f32[1,16,256]{2,1,0:T(8,128)S(1)} %get-tuple-element.23), channel_id=1, source_target_pairs={{4,0},{8,4},{12,8},{16,12},{20,16},{24,20},{28,24},{5,1},{9,5},{13... | collective-permute-start | bytes 49160 | tf_op jit(solution)/shard_map/ppermute | solution.py:20
  269.5 9.3 %copy-start.3 = (s32[64,16,256]{2,1,0:T(8,128)S(1)}, s32[64,16,256]{2,1,0:T(8,128)}, u32[]{:S(2)}) copy-start(s32[64,16,256]{2,1,0:T(8,128)} %param.10) | copy-start | bytes 3145732
  269.6 6.4 %collective-permute-start.6 = (f32[66,1,256]{2,0,1:T(8,128)S(1)}, f32[66,1,256]{2,0,1:T(8,128)S(1)}, u32[]{:S(2)}, u32[]{:S(2)}) collective-permute-start(f32[66,1,256]{2,0,1:T(8,128)S(1)} %copy.29), channel_id=1, source_target_pairs={{1,0},{2,1},{3,2},{5,4},{6,5},{7,6},{9,8},{10,9},{11,10},{13,12},{... | collective-permute-start | bytes 202760 | tf_op jit(solution)/shard_map/ppermute | solution.py:20
  271.0 6.5 %collective-permute-start.7 = (f32[66,1,256]{2,0,1:T(8,128)S(1)}, f32[66,1,256]{2,0,1:T(8,128)S(1)}, u32[]{:S(2)}, u32[]{:S(2)}) collective-permute-start(f32[66,1,256]{2,0,1:T(8,128)S(1)} %copy.31), channel_id=1, source_target_pairs={{0,1},{1,2},{2,3},{4,5},{5,6},{6,7},{8,9},{9,10},{10,11},{12,13},{... | collective-permute-start | bytes 202760 | tf_op jit(solution)/shard_map/ppermute | solution.py:17
  329.2 1.0 copy-start.4
Sparse Core Ops, SparseCore 0:
  13.5 37.6 reduce-scatter.1
  467.1 34.8 all-reduce.5
